TPU v7x, 32 devices: a whole 2x2x4 slice. The times are simulated.
32 devices in a mesh: dp: 4 (over z), ctx: 4 (over y, core), tensor: 2 (over x).
Axes of the slice: x: 2, y: 2, z: 4, core: 2. Of those that a mesh axis runs over, the one named last changes fastest.
Arguments:
- inputs: bfloat16 [4, 1024, 2048], P('dp', 'ctx'), may hold values from -6 to 6
- segments: int32 [4, 1024], P('dp'), may hold values from 0 to 4, as said below
- first_gain: bfloat16 [2048], replicated, may hold values from 0.5 to 1.5
- first_shift: bfloat16 [2048], replicated, may hold values from -3 to 3
- in_weight: bfloat16 [2048, 3, 2048], P(None, None, 'tensor'), may hold values from -0.125 to 0.125
- in_bias: bfloat16 [2, 2048], P(None, 'tensor'), may hold values from -2 to 2
- out_weight: bfloat16 [2048, 2048], P(None, 'tensor'), may hold values from -1 to 1
- out_bias: bfloat16 [2048], replicated, may hold values from -2 to 2
- second_gain: bfloat16 [2048], replicated, may hold values from 0.5 to 1.5
- second_shift: bfloat16 [2048], replicated, may hold values from -3 to 3
- up_weight: bfloat16 [2048, 8192], P(None, 'tensor'), may hold values from -0.125 to 0.125
- up_bias: bfloat16 [8192], P('tensor'), may hold values from -3 to 3
- down_weight: bfloat16 [2048, 8192], P(None, 'tensor'), may hold values from -0.0625 to 0.0625
- down_bias: bfloat16 [2048], replicated, may hold values from -2 to 2
- cotangent: bfloat16 [4, 1024, 2048], P('dp', 'ctx'), may hold values from -6 to 6
Outputs:
- outputs: bfloat16 [4, 1024, 2048], P('dp', ('ctx', 'tensor'))
- input_grad: bfloat16 [4, 1024, 2048], P('dp', ('ctx', 'tensor'))
- first_gain_grad: float32 [2048], replicated
- first_shift_grad: float32 [2048], replicated
- in_weight_grad: float32 [2048, 3, 2048], P(('dp', 'ctx'), None, 'tensor')
- in_bias_grad: float32 [2, 2048], P(None, 'tensor')
- out_weight_grad: float32 [2048, 2048], P(('dp', 'ctx'), 'tensor')
- out_bias_grad: float32 [2048], replicated
- second_gain_grad: float32 [2048], replicated
- second_shift_grad: float32 [2048], replicated
- up_weight_grad: float32 [2048, 8192], P(('dp', 'ctx'), 'tensor')
- up_bias_grad: float32 [8192], P('tensor')
- down_weight_grad: float32 [2048, 8192], P(('dp', 'ctx'), 'tensor')
- down_bias_grad: float32 [2048], replicated
Inputs may be any that keep to these rules, and one draw needn't show every extreme that they name: `segments`: along each sequence the numbers start at 0 and rise by one at each document boundary; every sequence holds exactly five documents.
All inputs are finite; a program needn't handle non-finite values.
Results may differ from a plain program's by a relative error of at most 0.019.
Values may be sent and summed in bfloat16 or wider, within the bound.
No kernel may reach another device: no remote copies, remote signals or barrier semaphores. Data moves between devices by JAX's collectives and lax.ppermute only.
A program may use at most 192 MiB of HBM per device.

v0:
```python
import math
import jax
import jax.numpy as jnp
from jax import lax
from jax.sharding import PartitionSpec as P

H = 16
HD = 128
EPSILON = 1e-05


def layer_norm(values, norm_gain, norm_shift):
    average = jnp.mean(values, axis=-1, keepdims=True)
    centered = values - average
    spread = jnp.mean(centered * centered, axis=-1, keepdims=True)
    return centered * lax.rsqrt(spread + EPSILON) * norm_gain + norm_shift


def contract(left, right, left_dim, right_dim):
    return lax.dot_general(
        left, right, (((left_dim,), (right_dim,)), ((), ())), preferred_element_type=jnp.float32
    )


def gelu_tanh(values):
    return jax.nn.gelu(values, approximate=True)


def shards(
    inputs,
    segments,
    first_gain,
    first_shift,
    in_weight,
    in_bias,
    out_weight,
    out_bias,
    second_gain,
    second_shift,
    up_weight,
    up_bias,
    down_weight,
    down_bias,
    cotangent,
):
    rows = inputs.shape[1]
    width = inputs.shape[2]
    local_width = in_weight.shape[2]
    local_hidden = up_weight.shape[1]
    heads_here = local_width // HD
    seq_length = segments.shape[1]
    share = rows // lax.axis_size("tensor")
    tensor_place = lax.axis_index("tensor")
    share_start = tensor_place * share
    scale = 1.0 / math.sqrt(HD)
    context_place = lax.axis_index("ctx")
    first_head = (tensor_place * heads_here).astype(jnp.float32)
    slopes = jnp.exp2(-8.0 * (first_head + jnp.arange(heads_here, dtype=jnp.float32) + 1.0) / H)
    segment_row = segments[0]
    query_pos = context_place * rows + jnp.arange(rows, dtype=jnp.int32)
    query_seg = lax.dynamic_slice_in_dim(segment_row, context_place * rows, rows)
    residual = inputs[0].astype(jnp.float32)
    residual_share = lax.dynamic_slice_in_dim(residual, share_start, share, 0)
    first_norm = (first_gain.astype(jnp.float32), first_shift.astype(jnp.float32))
    second_norm = (second_gain.astype(jnp.float32), second_shift.astype(jnp.float32))
    normed_first = layer_norm(residual, first_norm[0], first_norm[1]).astype(jnp.bfloat16)
    projected = jnp.einsum(
        "td,dcf->tcf", normed_first, in_weight, preferred_element_type=jnp.float32
    )
    bias_pair = in_bias.astype(jnp.float32)
    query_grid = (projected[:, 0] + bias_pair[0]).astype(jnp.bfloat16).reshape(rows, heads_here, HD)
    key_grid = projected[:, 1].astype(jnp.bfloat16).reshape(rows, heads_here, HD)
    value_grid = (projected[:, 2] + bias_pair[1]).astype(jnp.bfloat16).reshape(rows, heads_here, HD)
    keys_all, values_all = (
        lax.all_gather(key_grid, "ctx", axis=0, tiled=True),
        lax.all_gather(value_grid, "ctx", axis=0, tiled=True),
    )
    key_block = min(seq_length, max(rows, 512))
    needed = keys_all.shape[0] // key_block

    def block_scores(block):
        start = block * key_block
        key_part = lax.dynamic_slice_in_dim(keys_all, start, key_block, 0)
        value_part = lax.dynamic_slice_in_dim(values_all, start, key_block, 0)
        key_pos = start + jnp.arange(key_block, dtype=jnp.int32)
        key_seg = lax.dynamic_slice_in_dim(segment_row, start, key_block)
        raw = (
            jnp.einsum("qhd,khd->hqk", query_grid, key_part, preferred_element_type=jnp.float32)
            * scale
        )
        offset = (key_pos[None, :] - query_pos[:, None]).astype(jnp.float32)
        raw = raw + slopes[:, None, None] * offset[None]
        allowed = (
            (key_pos[None, :] <= query_pos[:, None]) & (key_seg[None, :] == query_seg[:, None])
        )[None]
        return (jnp.where(allowed, raw, -1e30), allowed, start, key_part, value_part)

    def stats_step(block, carry):
        top, total = carry
        scores, allowed, start, key_part, value_part = block_scores(block)
        new_top = jnp.maximum(top, jnp.max(scores, axis=-1))
        fresh = jnp.where(allowed, jnp.exp(scores - new_top[:, :, None]), 0.0)
        return (new_top, total * jnp.exp(top - new_top) + jnp.sum(fresh, axis=-1))

    start_top = jnp.full((heads_here, rows), -1e30, jnp.float32)
    start_total = jnp.zeros((heads_here, rows), jnp.float32)
    top, total = lax.fori_loop(0, needed, stats_step, (start_top, start_total))

    def probs_for(scores, allowed):
        return jnp.where(allowed, jnp.exp(scores - top[:, :, None]), 0.0) / total[:, :, None]

    def mix_step(block, carry):
        high_part, rest_part = carry
        scores, allowed, start, key_part, value_part = block_scores(block)
        probs = probs_for(scores, allowed)
        probs_low = lax.optimization_barrier(probs.astype(jnp.bfloat16))
        rest_low = (probs - probs_low.astype(jnp.float32)).astype(jnp.bfloat16)
        high_part = high_part + jnp.einsum(
            "hqk,khd->qhd", probs_low, value_part, preferred_element_type=jnp.float32
        )
        rest_part = rest_part + jnp.einsum(
            "hqk,khd->qhd", rest_low, value_part, preferred_element_type=jnp.float32
        )
        return (high_part, rest_part)

    empty_mix = jnp.zeros((rows, heads_here, HD), jnp.float32)
    mixed_high, mixed_rest = lax.fori_loop(0, needed, mix_step, (empty_mix, empty_mix))
    mixed_exact = (mixed_high + mixed_rest).reshape(rows, local_width)
    mixed_low = mixed_high.reshape(rows, local_width).astype(jnp.bfloat16)
    attention_share = lax.psum_scatter(
        contract(mixed_low, out_weight, 1, 1).astype(jnp.bfloat16),
        "tensor",
        scatter_dimension=0,
        tiled=True,
    ).astype(jnp.float32)
    middle_share = residual_share + attention_share + out_bias.astype(jnp.float32)
    normed_share, second_pull = jax.vjp(layer_norm, middle_share, second_norm[0], second_norm[1])
    normed_second = lax.all_gather(normed_share.astype(jnp.bfloat16), "tensor", axis=0, tiled=True)
    upper = jnp.dot(normed_second, up_weight, preferred_element_type=jnp.float32) + up_bias.astype(
        jnp.float32
    )
    active_full, gelu_pull = jax.vjp(gelu_tanh, upper)
    active = active_full.astype(jnp.bfloat16)
    feed_share = lax.psum_scatter(
        contract(active, down_weight, 1, 1).astype(jnp.bfloat16),
        "tensor",
        scatter_dimension=0,
        tiled=True,
    ).astype(jnp.float32)
    outputs = (middle_share + feed_share + down_bias.astype(jnp.float32)).astype(jnp.bfloat16)
    cotangent_low = cotangent[0]
    cotangent_share = lax.dynamic_slice_in_dim(cotangent_low, share_start, share, 0).astype(
        jnp.float32
    )
    down_whole = contract(cotangent_low, active, 0, 0)
    down_bias_term = jnp.sum(cotangent_share, axis=0)
    grad_active = jnp.dot(cotangent_low, down_weight, preferred_element_type=jnp.float32)
    grad_upper = gelu_pull(grad_active)[0].astype(jnp.bfloat16)
    up_bias_term = jnp.sum(grad_upper.astype(jnp.float32), axis=0)
    up_whole = contract(normed_second, grad_upper, 0, 0)
    grad_normed_share = lax.psum_scatter(
        contract(grad_upper, up_weight, 1, 1).astype(jnp.bfloat16),
        "tensor",
        scatter_dimension=0,
        tiled=True,
    ).astype(jnp.float32)
    grad_from_second, second_gain_term, second_shift_term = second_pull(grad_normed_share)
    grad_middle_share = cotangent_share + grad_from_second
    out_bias_term = jnp.sum(grad_middle_share, axis=0)
    grad_middle_low = lax.all_gather(
        grad_middle_share.astype(jnp.bfloat16), "tensor", axis=0, tiled=True
    )
    grad_mixed = jnp.dot(grad_middle_low, out_weight, preferred_element_type=jnp.float32).astype(
        jnp.bfloat16
    )
    out_whole = contract(grad_middle_low, mixed_low, 0, 0)
    delta = jnp.sum(
        (grad_mixed.astype(jnp.float32) * mixed_exact).reshape(rows, heads_here, HD), axis=-1
    ).T
    grad_mixed_grid = grad_mixed.reshape(rows, heads_here, HD)

    def back_step(block, carry):
        grad_query, grad_keys, grad_values = carry
        scores, allowed, start, key_part, value_part = block_scores(block)
        probs = probs_for(scores, allowed)
        probs_low = probs.astype(jnp.bfloat16)
        grad_probs = jnp.einsum(
            "qhd,khd->hqk", grad_mixed_grid, value_part, preferred_element_type=jnp.float32
        )
        grad_scores = (probs * (grad_probs - delta[:, :, None])).astype(jnp.bfloat16)
        grad_query = (
            grad_query
            + jnp.einsum("hqk,khd->qhd", grad_scores, key_part, preferred_element_type=jnp.float32)
            * scale
        )
        key_term = (
            jnp.einsum("hqk,qhd->khd", grad_scores, query_grid, preferred_element_type=jnp.float32)
            * scale
        )
        value_term = jnp.einsum(
            "hqk,qhd->khd", probs_low, grad_mixed_grid, preferred_element_type=jnp.float32
        )
        grad_keys = lax.dynamic_update_slice_in_dim(
            grad_keys, lax.dynamic_slice_in_dim(grad_keys, start, key_block, 0) + key_term, start, 0
        )
        grad_values = lax.dynamic_update_slice_in_dim(
            grad_values,
            lax.dynamic_slice_in_dim(grad_values, start, key_block, 0) + value_term,
            start,
            0,
        )
        return (grad_query, grad_keys, grad_values)

    empty_keys = jnp.zeros((keys_all.shape[0], heads_here, HD), jnp.float32)
    grad_query, grad_keys, grad_values = lax.fori_loop(
        0, needed, back_step, (empty_mix, empty_keys, empty_keys)
    )
    key_grad_part, value_grad_part = (
        lax.psum_scatter(
            grad_keys.astype(jnp.bfloat16), "ctx", scatter_dimension=0, tiled=True
        ).astype(jnp.float32),
        lax.psum_scatter(
            grad_values.astype(jnp.bfloat16), "ctx", scatter_dimension=0, tiled=True
        ).astype(jnp.float32),
    )
    grad_projected = jnp.stack(
        [
            grad_query.reshape(rows, local_width),
            key_grad_part.reshape(rows, local_width),
            value_grad_part.reshape(rows, local_width),
        ],
        axis=1,
    ).astype(jnp.bfloat16)
    in_bias_term = jnp.sum(grad_projected[:, 0::2].astype(jnp.float32), axis=0)
    in_whole = jnp.einsum(
        "td,tcf->dcf", normed_first, grad_projected, preferred_element_type=jnp.float32
    )
    grad_first_share = lax.psum_scatter(
        jnp.einsum(
            "tcf,dcf->td", grad_projected, in_weight, preferred_element_type=jnp.float32
        ).astype(jnp.bfloat16),
        "tensor",
        scatter_dimension=0,
        tiled=True,
    ).astype(jnp.float32)
    normed_again, first_pull = jax.vjp(layer_norm, residual_share, first_norm[0], first_norm[1])
    grad_from_first, first_gain_term, first_shift_term = first_pull(grad_first_share)
    input_grad = (grad_middle_share + grad_from_first).astype(jnp.bfloat16)
    in_weight_grad, out_weight_grad, up_weight_grad, down_weight_grad = (
        lax.psum_scatter(
            in_whole.astype(jnp.bfloat16), ("dp", "ctx"), scatter_dimension=0, tiled=True
        ).astype(jnp.float32),
        lax.psum_scatter(
            out_whole.astype(jnp.bfloat16), ("dp", "ctx"), scatter_dimension=0, tiled=True
        ).astype(jnp.float32),
        lax.psum_scatter(
            up_whole.astype(jnp.bfloat16), ("dp", "ctx"), scatter_dimension=0, tiled=True
        ).astype(jnp.float32),
        lax.psum_scatter(
            down_whole.astype(jnp.bfloat16), ("dp", "ctx"), scatter_dimension=0, tiled=True
        ).astype(jnp.float32),
    )
    in_bias_whole = lax.dynamic_update_slice(
        jnp.zeros((2, width), jnp.float32), in_bias_term, (0, tensor_place * local_width)
    )
    up_bias_whole = lax.dynamic_update_slice(
        jnp.zeros((local_hidden * lax.axis_size("tensor"),), jnp.float32),
        up_bias_term,
        (tensor_place * local_hidden,),
    )
    small_sums = lax.psum(
        (
            first_gain_term,
            first_shift_term,
            in_bias_whole,
            out_bias_term,
            second_gain_term,
            second_shift_term,
            up_bias_whole,
            down_bias_term,
        ),
        ("dp", "ctx", "tensor"),
    )
    in_bias_grad = lax.dynamic_slice_in_dim(
        small_sums[2], tensor_place * local_width, local_width, 1
    )
    up_bias_grad = lax.dynamic_slice_in_dim(
        small_sums[6], tensor_place * local_hidden, local_hidden, 0
    )
    return (
        outputs[None],
        input_grad[None],
        small_sums[0],
        small_sums[1],
        in_weight_grad,
        in_bias_grad,
        out_weight_grad,
        small_sums[3],
        small_sums[4],
        small_sums[5],
        up_weight_grad,
        up_bias_grad,
        down_weight_grad,
        small_sums[7],
    )


def solution(mesh):
    return jax.shard_map(
        shards,
        mesh=mesh,
        in_specs=(
            P("dp", "ctx", None),
            P("dp", None),
            P(),
            P(),
            P(None, None, "tensor"),
            P(None, "tensor"),
            P(None, "tensor"),
            P(),
            P(),
            P(),
            P(None, "tensor"),
            P("tensor"),
            P(None, "tensor"),
            P(),
            P("dp", "ctx", None),
        ),
        out_specs=(
            P("dp", ("ctx", "tensor"), None),
            P("dp", ("ctx", "tensor"), None),
            P(),
            P(),
            P(("dp", "ctx"), None, "tensor"),
            P(None, "tensor"),
            P(("dp", "ctx"), "tensor"),
            P(),
            P(),
            P(),
            P(("dp", "ctx"), "tensor"),
            P("tensor"),
            P(("dp", "ctx"), "tensor"),
            P(),
        ),
        check_vma=False,
    )
```

profile of v0, /device:TPU:0, one launch (start us, length us, event | category | flops | bytes accessed | tf_op | source)
XLA Modules:
  0.0 1117.3 jit_solution(4887311695506873772)
XLA Ops:
  11.7 7.0 fusion.87
  25.9 21.1 %all-gather.7.cloned.1.call-done = bf16[1024,8,128]{2,0,1:T(8,128)(2,1)} async-done(((bf16[256,8,128]{2,0,1:T(8,128)(2,1)}), bf16[1024,8,128]{2,0,1:T(8,128)(2,1)}) %all-gather.7.cloned.1.call-update) | async-done | bytes 2097168 | tf_op jit(solution)/shard_map/all_gather | solution.py:75
  47.0 16.6 %while.50 = (s32[]{:T(128)}, f32[8,256]{1,0:T(8,128)S(1)}, f32[8,256]{1,0:T(8,128)S(1)}, s32[1024]{0:T(1024)S(1)}, s32[256]{0:T(256)S(1)}, /*index=5*/bf16[1024,...) while((s32[]{:T(128)}, f32[8,256]{1,0:T(8,128)S(1)}, ...), condition=%wide.region_5.6_spmd.clone, body=%wide.region_2.5_spmd.clone.sunk | while | flops 281684768 | bytes 12050738 | solution.py:107
  55.7 4.3 fusion.148
  63.6 8.1 all-gather.5.cloned.1.call-done
  71.7 25.1 %while.51 = (s32[]{:T(128)}, f32[256,8,128]{0,2,1:T(8,128)}, f32[256,8,128]{0,2,1:T(8,128)S(1)}, bf16[1024,8,128]{2,0,1:T(8,128)(2,1)}, s32[1024]{0:T(1024)S(1)}...) while((s32[]{:T(128)}, f32[256,8,128]{0,2,1:T(8,128)}, ...), condition=%wide.region_7.8_spmd.clone, body=%wide.region_6.7_spmd.clone.sunk | while | flops 818545408 | bytes 32276812 | solution.py:127
  73.0 5.1 fusion.154
  85.4 5.1 fusion.154
  99.5 4.7 convolution_convert_fusion.5
  104.8 19.9 %reduce-scatter.13.cloned.1.call-done = bf16[128,2048]{1,0:T(8,128)(2,1)} async-done(((bf16[256,2048]{1,0:T(8,128)(2,1)}), bf16[128,2048]{1,0:T(8,128)(2,1)}) %reduce-scatter.13.cloned.1.call-update) | async-done | bytes 524304 | tf_op jit(solution)/shard_map/reduce_scatter | solution.py:130
  127.4 21.4 %all-gather.9.cloned.1.call-done = bf16[256,2048]{1,0:T(8,128)(2,1)} async-done(((bf16[128,2048]{1,0:T(8,128)(2,1)}), bf16[256,2048]{1,0:T(8,128)(2,1)}) %all-gather.9.cloned.1.call-update) | async-done | bytes 1048592 | tf_op jit(solution)/shard_map/all_gather | solution.py:138
  148.8 8.5 convolution_add_fusion
  157.3 12.7 %convert_reduce_fusion = (f32[4096]{0:T(1024)S(1)}, bf16[256,4096]{1,0:T(8,128)(2,1)}) fusion(f32[256,4096]{1,0:T(8,128)S(1)} %convolution_add_fusion, bf16[2048,4096]{1,0:T(8,128)(2,1)} %param.33, bf16[1,256,2048]{2,1,0:T(8,128)(2,1)S(1)} %copy-done.22), kind=kOutput, calls=%fused_computation.85 | convolution fusion | flops 4318031872 | bytes 24133632 | tf_op jit(solution)/shard_map/dot_general | solution.py:157
  170.0 11.9 %convolution_convert_fusion.3 = bf16[256,2048]{1,0:T(8,128)(2,1)} fusion(bf16[256,4096]{1,0:T(8,128)(2,1)} %get-tuple-element.946, bf16[2048,4096]{1,0:T(8,128)(2,1)} %param.31), kind=kOutput, calls=%fused_computation.89 | convolution fusion | flops 4295491584 | bytes 19922944 | tf_op jit(solution)/shard_map/dot_general | solution.py:20
  182.2 13.3 %convolution_convert_fusion.4 = bf16[256,2048]{1,0:T(8,128)(2,1)} fusion(bf16[2048,4096]{1,0:T(8,128)(2,1)} %param.33, f32[256,4096]{1,0:T(8,128)} %copy-done.47), kind=kOutput, calls=%fused_computation.90 | convolution fusion | flops 4304928768 | bytes 22020096 | tf_op jit(solution)/shard_map/dot_general | solution.py:20
  195.7 6.8 reduce-scatter.17.cloned.1.call-done
  206.7 18.2 %reduce-scatter.15.cloned.1.call-done = bf16[128,2048]{1,0:T(8,128)(2,1)} async-done(((bf16[256,2048]{1,0:T(8,128)(2,1)}), bf16[128,2048]{1,0:T(8,128)(2,1)}) %reduce-scatter.15.cloned.1.call-update) | async-done | bytes 524304 | tf_op jit(solution)/shard_map/reduce_scatter | solution.py:144
  230.6 20.8 %all-gather.11.cloned.1.call-done = bf16[256,2048]{1,0:T(8,128)(2,1)} async-done(((bf16[128,2048]{1,0:T(8,128)(2,1)}), bf16[256,2048]{1,0:T(8,128)(2,1)}) %all-gather.11.cloned.1.call-update) | async-done | bytes 1048592 | tf_op jit(solution)/shard_map/all_gather | solution.py:170
  260.6 32.2 %while.52 = (s32[]{:T(128)}, f32[256,8,128]{0,2,1:T(8,128)}, f32[1024,8,128]{2,0,1:T(8,128)}, f32[1024,8,128]{2,0,1:T(8,128)}, bf16[1024,8,128]{2,0,1:T(8,128)(2...) while((s32[]{:T(128)}, f32[256,8,128]{0,2,1:T(8,128)}, ...), condition=%wide.region_17.18_spmd.clone, body=%wide.region_16.17_spmd.clone.sunk | while | flops 1356727040 | bytes 111452632 | solution.py:215
  301.6 26.7 %reduce-scatter.21.cloned.1.call-done = bf16[256,8,128]{2,0,1:T(8,128)(2,1)} async-done(((bf16[1024,8,128]{2,0,1:T(8,128)(2,1)}), bf16[256,8,128]{2,0,1:T(8,128)(2,1)}) %reduce-scatter.21.cloned.1.call-update) | async-done | bytes 524304 | tf_op jit(solution)/shard_map/reduce_scatter | solution.py:222
  329.9 32.4 %reduce-scatter.19.cloned.1.call-done = bf16[256,8,128]{2,0,1:T(8,128)(2,1)} async-done(((bf16[1024,8,128]{2,0,1:T(8,128)(2,1)}), bf16[256,8,128]{2,0,1:T(8,128)(2,1)}) %reduce-scatter.19.cloned.1.call-update) | async-done | bytes 524304 | tf_op jit(solution)/shard_map/reduce_scatter | solution.py:219
  364.0 9.2 fusion.60
  381.9 11.7 %reduce-scatter.23.cloned.1.call-done = bf16[128,2048]{1,0:T(8,128)(2,1)} async-done(((bf16[256,2048]{1,0:T(8,128)(2,1)}), bf16[128,2048]{1,0:T(8,128)(2,1)}) %reduce-scatter.23.cloned.1.call-update) | async-done | bytes 524304 | tf_op jit(solution)/shard_map/reduce_scatter | solution.py:238
  398.1 14.2 %convert_bitcast_fusion = bf16[2048,4096]{0,1:T(8,128)(2,1)} fusion(bf16[1,256,2048]{2,1,0:T(8,128)(2,1)} %param.35, f32[256,4096]{1,0:T(8,128)} %copy-done.47), kind=kOutput, calls=%fused_computation.72 | convolution fusion | flops 4312793088 | bytes 22020096 | tf_op jit(solution)/shard_map/dot_general | solution.py:20
  412.3 21.6 %copy.68 = bf16[2048,4096]{1,0:T(8,128)(2,1)} copy(bf16[2048,4096]{0,1:T(8,128)(2,1)} %convert_bitcast_fusion) | data formatting | bytes 33554432
  435.2 9.9 convolution_convert_fusion
  446.3 7.9 convolution_convert_fusion.1
  454.3 15.7 %reduce-scatter.27.cloned.1.call-done = bf16[128,1024]{1,0:T(8,128)(2,1)} async-done(((bf16[2048,1024]{1,0:T(8,128)(2,1)}), bf16[128,1024]{1,0:T(8,128)(2,1)}) %reduce-scatter.27.cloned.1.call-update) | async-done | bytes 262160 | tf_op jit(solution)/shard_map/reduce_scatter | solution.py:253
  474.1 127.4 %all-reduce.3.cloned.1.call-done = (f32[2048]{0:T(1024)}, f32[2048]{0:T(1024)}, f32[2,2048]{1,0:T(2,128)}, f32[2048]{0:T(1024)}, f32[2048]{0:T(1024)}, /*index=5*/f32[2048]{0:T(1024)}, f32[8192]{0:T(1024)}, f32[2048]{0:T(1024)}) async-done(((f32[2048]{0:T(1024)}, f32[2048]{0:T(1024)}, f32[2,2048]{1,0:T(2,128)}, f32[2048]{0:T(1024)}, f32[2048]{0:T(1024)}, /*index=5*/f32[2048]{0:T(1024)}, f32[8192]{0:T(1024)}, ...) | async-done | bytes 98320 | tf_op jit(solution)/shard_map/psum | solution.py:271
  604.1 181.2 %reduce-scatter.31.cloned.1.call-done = bf16[128,4096]{1,0:T(8,128)(2,1)} async-done(((bf16[2048,4096]{1,0:T(8,128)(2,1)}), bf16[128,4096]{1,0:T(8,128)(2,1)}) %reduce-scatter.31.cloned.1.call-update) | async-done | bytes 1048592
  788.5 178.3 %reduce-scatter.29.cloned.1.call-done = bf16[128,4096]{1,0:T(8,128)(2,1)} async-done(((bf16[2048,4096]{1,0:T(8,128)(2,1)}), bf16[128,4096]{1,0:T(8,128)(2,1)}) %reduce-scatter.29.cloned.1.call-update) | async-done | bytes 1048592 | tf_op jit(solution)/shard_map/reduce_scatter | solution.py:256
  969.6 134.9 %reduce-scatter.25.cloned.1.call-done = bf16[128,3,1024]{2,0,1:T(8,128)(2,1)} async-done(((bf16[2048,3,1024]{2,0,1:T(8,128)(2,1)}), bf16[128,3,1024]{2,0,1:T(8,128)(2,1)}) %reduce-scatter.25.cloned.1.call-update) | async-done | bytes 786448 | tf_op jit(solution)/shard_map/reduce_scatter | solution.py:250
  (281 shorter events, 142.1 us)
Async XLA Ops:
  7.2 39.8 %all-gather.7.cloned.1.call-start = ((), (), s32[]{:S(2)}) async-start(), calls=%async_computation.11 | async-start | bytes 2621440 | tf_op jit(solution)/shard_map/all_gather | solution.py:75
  21.5 50.2 %all-gather.5.cloned.1.call-start = ((), (), s32[]{:S(2)}) async-start(), calls=%async_computation.10 | async-start | bytes 2621440 | tf_op jit(solution)/shard_map/all_gather | solution.py:76
  24.5 100.2 %reduce-scatter.13.cloned.1.call-start = ((), (), s32[]{:S(2)}) async-start(), calls=%async_computation.12 | async-start | bytes 1572864 | tf_op jit(solution)/shard_map/reduce_scatter | solution.py:130
  104.2 23.1 %copy-start.30 = (bf16[4096]{0:T(1024)(128)(2,1)S(1)}, bf16[4096]{0:T(1024)(128)(2,1)}, u32[]{:S(2)}) copy-start(bf16[4096]{0:T(1024)(128)(2,1)} %param.32) | copy-start | bytes 24580
  104.2 44.5 %all-gather.9.cloned.1.call-start = ((), (), s32[]{:S(2)}) async-start(), calls=%async_computation.13 | async-start | bytes 1572864 | tf_op jit(solution)/shard_map/all_gather | solution.py:138
  104.7 52.6 %copy-start.7 = (f32[1,256,2048]{2,1,0:T(8,128)}, f32[1,256,2048]{2,1,0:T(8,128)S(1)}, u32[]{:S(2)}) copy-start(f32[1,256,2048]{2,1,0:T(8,128)S(1)} %convert_element_type.219) | copy-start | bytes 6291460
  127.3 75.1 %reduce-scatter.17.cloned.1.call-start = ((), (), s32[]{:S(2)}) async-start(), calls=%async_computation.15 | async-start | bytes 1572864 | tf_op jit(solution)/shard_map/reduce_scatter | solution.py:161
  182.0 13.7 %copy-start.42 = (bf16[2048]{0:T(1024)(128)(2,1)S(1)}, bf16[2048]{0:T(1024)(128)(2,1)}, u32[]{:S(2)}) copy-start(bf16[2048]{0:T(1024)(128)(2,1)} %param.34) | copy-start | bytes 12292
  182.0 42.9 %reduce-scatter.15.cloned.1.call-start = ((), (), s32[]{:S(2)}) async-start(), calls=%async_computation.14 | async-start | bytes 1572864 | tf_op jit(solution)/shard_map/reduce_scatter | solution.py:144
  195.6 29.3 %copy-start.23 = (bf16[1,256,2048]{2,1,0:T(8,128)(2,1)S(1)}, bf16[1,256,2048]{2,1,0:T(8,128)(2,1)}, u32[]{:S(2)}) copy-start(bf16[1,256,2048]{2,1,0:T(8,128)(2,1)} %param.35) | copy-start | bytes 3145732
  195.6 55.8 %all-gather.11.cloned.1.call-start = ((), (), s32[]{:S(2)}) async-start(), calls=%async_computation.16 | async-start | bytes 1572864 | tf_op jit(solution)/shard_map/all_gather | solution.py:170
  204.4 25.8 %copy-start.13 = (f32[256,8,128]{0,2,1:T(8,128)S(1)}, f32[256,8,128]{0,2,1:T(8,128)}, u32[]{:S(2)}) copy-start(f32[256,8,128]{0,2,1:T(8,128)} %get-tuple-element.938) | copy-start | bytes 3145732
  229.9 98.4 %reduce-scatter.21.cloned.1.call-start = ((), (), s32[]{:S(2)}) async-start(), calls=%async_computation.18 | async-start | bytes 2621440 | tf_op jit(solution)/shard_map/reduce_scatter | solution.py:222
  296.7 65.6 %reduce-scatter.19.cloned.1.call-start = ((), (), s32[]{:S(2)}) async-start(), calls=%async_computation.17 | async-start | bytes 2621440 | tf_op jit(solution)/shard_map/reduce_scatter | solution.py:219
  300.8 92.9 %reduce-scatter.23.cloned.1.call-start = ((), (), s32[]{:S(2)}) async-start(), calls=%async_computation.19 | async-start | bytes 1572864 | tf_op jit(solution)/shard_map/reduce_scatter | solution.py:238
  301.6 78.8 %copy-start.18 = (bf16[256,1,1024]{2,0,1:T(8,128)(2,1)}, bf16[256,1,1024]{2,0,1:T(8,128)(2,1)S(1)}, u32[]{:S(2)}) copy-start(bf16[256,1,1024]{2,0,1:T(8,128)(2,1)S(1)} %copy.66) | copy-start | bytes 1572868
  329.9 50.5 %copy-start.19 = (bf16[256,1,1024]{2,0,1:T(8,128)(2,1)}, bf16[256,1,1024]{2,0,1:T(8,128)(2,1)S(1)}, u32[]{:S(2)}) copy-start(bf16[256,1,1024]{2,0,1:T(8,128)(2,1)S(1)} %stack_reshape.14) | copy-start | bytes 1572868
  373.2 96.8 %reduce-scatter.27.cloned.1.call-start = ((), (), s32[]{:S(2)}) async-start(), calls=%async_computation.21 | async-start | bytes 4456448 | tf_op jit(solution)/shard_map/reduce_scatter | solution.py:253
  376.5 17.1 %copy-start.26 = (f32[2048]{0:T(1024)S(1)}, f32[2048]{0:T(1024)}, u32[]{:S(2)}) copy-start(f32[2048]{0:T(1024)} %copy-done.25) | copy-start | bytes 24580
  376.6 224.9 %all-reduce.3.cloned.1.call-start = ((), (), s32[]{:S(2)}) async-start(), calls=%async_computation.24 | async-start | bytes 196608 | tf_op jit(solution)/shard_map/psum | solution.py:271
  380.4 17.5 %copy-start.27 = (f32[8192]{0:T(1024)}, f32[8192]{0:T(1024)S(1)}, u32[]{:S(2)}) copy-start(f32[8192]{0:T(1024)S(1)} %dynamic_update_slice.21) | copy-start | bytes 98308
  381.9 16.0 %copy-start.28 = (f32[2,2048]{1,0:T(2,128)}, f32[2,2048]{1,0:T(2,128)S(1)}, u32[]{:S(2)}) copy-start(f32[2,2048]{1,0:T(2,128)S(1)} %constant_dynamic-update-slice_fusion) | copy-start | bytes 49156
  397.9 387.3 %reduce-scatter.31.cloned.1.call-start = ((), (), s32[]{:S(2)}) async-start(), calls=%async_computation.23 | async-start | bytes 17825792
  434.0 532.8 %reduce-scatter.29.cloned.1.call-start = ((), (), s32[]{:S(2)}) async-start(), calls=%async_computation.22 | async-start | bytes 17825792 | tf_op jit(solution)/shard_map/reduce_scatter | solution.py:256
  445.1 659.4 %reduce-scatter.25.cloned.1.call-start = ((), (), s32[]{:S(2)}) async-start(), calls=%async_computation.20 | async-start | bytes 13369344 | tf_op jit(solution)/shard_map/reduce_scatter | solution.py:250
  454.3 17.6 %copy-start.12 = (f32[128,2048]{1,0:T(8,128)S(1)}, f32[128,2048]{1,0:T(8,128)}, u32[]{:S(2)}) copy-start(f32[128,2048]{1,0:T(8,128)} %copy-done.11) | copy-start | bytes 3145732
  786.8 320.1 %copy-start.38 = (f32[2048]{0:T(1024)S(1)}, f32[2048]{0:T(1024)}, u32[]{:S(2)}) copy-start(f32[2048]{0:T(1024)} %get-tuple-element.1320) | copy-start | bytes 24580
  786.9 320.7 %copy-start.37 = (f32[2048]{0:T(1024)S(1)}, f32[2048]{0:T(1024)}, u32[]{:S(2)}) copy-start(f32[2048]{0:T(1024)} %get-tuple-element.1321) | copy-start | bytes 24580
  786.9 321.3 %copy-start.36 = (f32[2048]{0:T(1024)S(1)}, f32[2048]{0:T(1024)}, u32[]{:S(2)}) copy-start(f32[2048]{0:T(1024)} %get-tuple-element.1325) | copy-start | bytes 24580
  786.9 321.9 %copy-start.35 = (f32[2048]{0:T(1024)S(1)}, f32[2048]{0:T(1024)}, u32[]{:S(2)}) copy-start(f32[2048]{0:T(1024)} %get-tuple-element.1326) | copy-start | bytes 24580
  786.9 322.5 %copy-start.34 = (f32[2048]{0:T(1024)S(1)}, f32[2048]{0:T(1024)}, u32[]{:S(2)}) copy-start(f32[2048]{0:T(1024)} %get-tuple-element.1327) | copy-start | bytes 24580
  786.9 323.1 %copy-start.33 = (f32[2048]{0:T(1024)S(1)}, f32[2048]{0:T(1024)}, u32[]{:S(2)}) copy-start(f32[2048]{0:T(1024)} %get-tuple-element.1331) | copy-start | bytes 24580
  (37 other events, 176.4 us)
Sparse Core Ops, SparseCore 0:
  21.6 25.2 all-gather.6
  49.1 22.5 all-gather.4
  104.3 20.3 reduce-scatter.12
  127.4 21.2 all-gather.8
  182.1 20.3 reduce-scatter.16
  204.5 20.3 reduce-scatter.14
  230.1 21.2 all-gather.10
  296.9 31.4 reduce-scatter.20
  330.9 31.4 reduce-scatter.18
  373.3 20.2 reduce-scatter.22
  397.5 72.4 reduce-scatter.26
  478.6 122.7 all-reduce.2
  605.5 179.6 reduce-scatter.30
  789.2 177.5 reduce-scatter.28
  970.7 133.7 reduce-scatter.24
where the time goes:
time: 1130 us; the launch traced here: 1120 us
  waiting for transfers between devices  825 us (73%)
  matrix products  161 us (14%)
  local copies, waits for them, and re-layouts  58.1 us (5%)
  other arithmetic  56.4 us (5%)
  between operations  14.9 us (1%)
    unnamed x16, waiting for transfers between devices  181 us
    reduce_scatter x1, waiting for transfers between devices, shards(): lax.psum_scatter(up_whole.astype(jnp.bfloat16), ('dp', 'ctx'), scatter_di...  178 us
    reduce_scatter x1, waiting for transfers between devices, shards(): lax.psum_scatter(in_whole.astype(jnp.bfloat16), ('dp', 'ctx'), scatter_di...  135 us
    psum x1, waiting for transfers between devices, shards(): lax.psum((first_gain_term, first_shift_term, in_bias_whole, out_bias_term...  127 us
    dot_general x6, matrix products, contract(): lax.dot_general(left, right, (((left_dim,), (right_dim,)), ((), ())), pre...  57.2 us
    unnamed x101, local copies, waits for them, and re-layouts  37.6 us
    reduce_scatter x1, waiting for transfers between devices, shards(): lax.psum_scatter(grad_keys.astype(jnp.bfloat16), 'ctx', scatter_dimension...  32.4 us
    reduce_scatter x1, waiting for transfers between devices, shards(): lax.psum_scatter(grad_values.astype(jnp.bfloat16), 'ctx', scatter_dimensi...  26.7 us
  transfers between devices with their start and end apart: 15, of which 15 were waited for; matrix products, arithmetic and copies ran while one was open for 11% of the time, Pallas kernels for 0%

commit v1 on v0

--- a/solution.py
+++ b/solution.py
@@ -269,17 +269,20 @@
         (tensor_place * local_hidden,),
     )
     small_sums = lax.psum(
-        (
-            first_gain_term,
-            first_shift_term,
-            in_bias_whole,
-            out_bias_term,
-            second_gain_term,
-            second_shift_term,
-            up_bias_whole,
-            down_bias_term,
+        lax.psum(
+            (
+                first_gain_term,
+                first_shift_term,
+                in_bias_whole,
+                out_bias_term,
+                second_gain_term,
+                second_shift_term,
+                up_bias_whole,
+                down_bias_term,
+            ),
+            ("ctx", "tensor"),
         ),
-        ("dp", "ctx", "tensor"),
+        "dp",
     )
     in_bias_grad = lax.dynamic_slice_in_dim(
         small_sums[2], tensor_place * local_width, local_width, 1

time: 1130 us -> 1090 us (0.965)
  waiting for transfers between devices: 825 us -> 792 us
    psum x1, waiting for transfers between devices: 127 us -> 49.7 us  [shards(): lax.psum((first_gain_term, first_shift_term, in_bias_whole, out_bias_term...]
    psum x0 -> x1, waiting for transfers between devices: none -> 32.9 us  [shards(): lax.psum(lax.psum((first_gain_term, first_shift_term, in_bias_whole, out_...]
    unnamed x101 -> x99, local copies, waits for them, and re-layouts: 37.6 us -> 36.2 us
    unnamed x16 -> x17, waiting for transfers between devices: 181 us -> 181 us
  transfers between devices with their start and end apart: 15 -> 16, of which waited for: 15 -> 16; matrix products, arithmetic and copies ran while one was open for 11% -> 11% of each run, Pallas kernels for 0% -> 0%
where the time goes in v1:
time: 1090 us; the launch traced here: 1080 us
  waiting for transfers between devices  792 us (73%)
  matrix products  159 us (15%)
  local copies, waits for them, and re-layouts  57.5 us (5%)
  other arithmetic  56.8 us (5%)
  between operations  14.8 us (1%)
    unnamed x17, waiting for transfers between devices  181 us
    reduce_scatter x1, waiting for transfers between devices, shards(): lax.psum_scatter(up_whole.astype(jnp.bfloat16), ('dp', 'ctx'), scatter_di...  179 us
    reduce_scatter x1, waiting for transfers between devices, shards(): lax.psum_scatter(in_whole.astype(jnp.bfloat16), ('dp', 'ctx'), scatter_di...  135 us
    dot_general x6, matrix products, contract(): lax.dot_general(left, right, (((left_dim,), (right_dim,)), ((), ())), pre...  55.5 us
    psum x1, waiting for transfers between devices, shards(): lax.psum((first_gain_term, first_shift_term, in_bias_whole, out_bias_term...  49.7 us
    unnamed x99, local copies, waits for them, and re-layouts  36.2 us
    psum x1, waiting for transfers between devices, shards(): lax.psum(lax.psum((first_gain_term, first_shift_term, in_bias_whole, out_...  32.9 us
    reduce_scatter x1, waiting for transfers between devices, shards(): lax.psum_scatter(grad_keys.astype(jnp.bfloat16), 'ctx', scatter_dimension...  32.4 us
  transfers between devices with their start and end apart: 16, of which 16 were waited for; matrix products, arithmetic and copies ran while one was open for 11% of the time, Pallas kernels for 0%

profile of v1, /device:TPU:0, one launch (start us, length us, event | category | flops | bytes accessed | tf_op | source)
XLA Modules:
  0.0 1083.2 jit_solution(11420607034312700475)
XLA Ops:
  11.7 7.0 fusion.87
  25.9 21.1 %all-gather.7.cloned.1.call-done = bf16[1024,8,128]{2,0,1:T(8,128)(2,1)} async-done(((bf16[256,8,128]{2,0,1:T(8,128)(2,1)}), bf16[1024,8,128]{2,0,1:T(8,128)(2,1)}) %all-gather.7.cloned.1.call-update) | async-done | bytes 2097168 | tf_op jit(solution)/shard_map/all_gather | solution.py:75
  47.0 16.7 %while.50 = (s32[]{:T(128)}, f32[8,256]{1,0:T(8,128)S(1)}, f32[8,256]{1,0:T(8,128)S(1)}, s32[1024]{0:T(1024)S(1)}, s32[256]{0:T(256)S(1)}, /*index=5*/bf16[1024,...) while((s32[]{:T(128)}, f32[8,256]{1,0:T(8,128)S(1)}, ...), condition=%wide.region_5.6_spmd.clone, body=%wide.region_2.5_spmd.clone.sunk | while | flops 281684768 | bytes 12050738 | solution.py:107
  63.7 8.1 all-gather.5.cloned.1.call-done
  71.7 25.1 %while.51 = (s32[]{:T(128)}, f32[256,8,128]{0,2,1:T(8,128)}, f32[256,8,128]{0,2,1:T(8,128)S(1)}, bf16[1024,8,128]{2,0,1:T(8,128)(2,1)}, s32[1024]{0:T(1024)S(1)}...) while((s32[]{:T(128)}, f32[256,8,128]{0,2,1:T(8,128)}, ...), condition=%wide.region_7.8_spmd.clone, body=%wide.region_6.7_spmd.clone.sunk | while | flops 818545408 | bytes 32276812 | solution.py:127
  73.0 5.1 fusion.154
  85.4 5.1 fusion.154
  99.6 4.7 convolution_convert_fusion.5
  104.8 19.9 %reduce-scatter.13.cloned.1.call-done = bf16[128,2048]{1,0:T(8,128)(2,1)} async-done(((bf16[256,2048]{1,0:T(8,128)(2,1)}), bf16[128,2048]{1,0:T(8,128)(2,1)}) %reduce-scatter.13.cloned.1.call-update) | async-done | bytes 524304 | tf_op jit(solution)/shard_map/reduce_scatter | solution.py:130
  127.4 21.4 %all-gather.9.cloned.1.call-done = bf16[256,2048]{1,0:T(8,128)(2,1)} async-done(((bf16[128,2048]{1,0:T(8,128)(2,1)}), bf16[256,2048]{1,0:T(8,128)(2,1)}) %all-gather.9.cloned.1.call-update) | async-done | bytes 1048592 | tf_op jit(solution)/shard_map/all_gather | solution.py:138
  148.8 8.5 convolution_add_fusion
  157.3 12.7 %convert_reduce_fusion = (f32[4096]{0:T(1024)S(1)}, bf16[256,4096]{1,0:T(8,128)(2,1)}) fusion(f32[256,4096]{1,0:T(8,128)S(1)} %convolution_add_fusion, bf16[2048,4096]{1,0:T(8,128)(2,1)} %param.33, bf16[1,256,2048]{2,1,0:T(8,128)(2,1)S(1)} %copy-done.20), kind=kOutput, calls=%fused_computation.85 | convolution fusion | flops 4318031872 | bytes 24133632 | tf_op jit(solution)/shard_map/dot_general | solution.py:157
  170.0 11.9 %convolution_convert_fusion.3 = bf16[256,2048]{1,0:T(8,128)(2,1)} fusion(bf16[256,4096]{1,0:T(8,128)(2,1)} %get-tuple-element.954, bf16[2048,4096]{1,0:T(8,128)(2,1)} %param.31), kind=kOutput, calls=%fused_computation.89 | convolution fusion | flops 4295491584 | bytes 19922944 | tf_op jit(solution)/shard_map/dot_general | solution.py:20
  182.2 13.3 %convolution_convert_fusion.4 = bf16[256,2048]{1,0:T(8,128)(2,1)} fusion(bf16[2048,4096]{1,0:T(8,128)(2,1)} %param.33, f32[256,4096]{1,0:T(8,128)} %copy-done.46), kind=kOutput, calls=%fused_computation.90 | convolution fusion | flops 4304928768 | bytes 22020096 | tf_op jit(solution)/shard_map/dot_general | solution.py:20
  195.7 6.8 reduce-scatter.17.cloned.1.call-done
  206.7 18.2 %reduce-scatter.15.cloned.1.call-done = bf16[128,2048]{1,0:T(8,128)(2,1)} async-done(((bf16[256,2048]{1,0:T(8,128)(2,1)}), bf16[128,2048]{1,0:T(8,128)(2,1)}) %reduce-scatter.15.cloned.1.call-update) | async-done | bytes 524304 | tf_op jit(solution)/shard_map/reduce_scatter | solution.py:144
  230.6 20.8 %all-gather.11.cloned.1.call-done = bf16[256,2048]{1,0:T(8,128)(2,1)} async-done(((bf16[128,2048]{1,0:T(8,128)(2,1)}), bf16[256,2048]{1,0:T(8,128)(2,1)}) %all-gather.11.cloned.1.call-update) | async-done | bytes 1048592 | tf_op jit(solution)/shard_map/all_gather | solution.py:170
  260.7 32.3 %while.52 = (s32[]{:T(128)}, f32[256,8,128]{0,2,1:T(8,128)}, f32[1024,8,128]{2,0,1:T(8,128)}, f32[1024,8,128]{2,0,1:T(8,128)}, bf16[1024,8,128]{2,0,1:T(8,128)(2...) while((s32[]{:T(128)}, f32[256,8,128]{0,2,1:T(8,128)}, ...), condition=%wide.region_17.18_spmd.clone, body=%wide.region_16.17_spmd.clone.sunk | while | flops 1356727040 | bytes 111452632 | solution.py:215
  301.7 26.7 %reduce-scatter.21.cloned.1.call-done = bf16[256,8,128]{2,0,1:T(8,128)(2,1)} async-done(((bf16[1024,8,128]{2,0,1:T(8,128)(2,1)}), bf16[256,8,128]{2,0,1:T(8,128)(2,1)}) %reduce-scatter.21.cloned.1.call-update) | async-done | bytes 524304 | tf_op jit(solution)/shard_map/reduce_scatter | solution.py:222
  330.1 32.4 %reduce-scatter.19.cloned.1.call-done = bf16[256,8,128]{2,0,1:T(8,128)(2,1)} async-done(((bf16[1024,8,128]{2,0,1:T(8,128)(2,1)}), bf16[256,8,128]{2,0,1:T(8,128)(2,1)}) %reduce-scatter.19.cloned.1.call-update) | async-done | bytes 524304 | tf_op jit(solution)/shard_map/reduce_scatter | solution.py:219
  364.8 9.3 fusion.60
  378.4 16.2 %reduce-scatter.23.cloned.1.call-done = bf16[128,2048]{1,0:T(8,128)(2,1)} async-done(((bf16[256,2048]{1,0:T(8,128)(2,1)}), bf16[128,2048]{1,0:T(8,128)(2,1)}) %reduce-scatter.23.cloned.1.call-update) | async-done | bytes 524304 | tf_op jit(solution)/shard_map/reduce_scatter | solution.py:238
  403.3 49.7 %all-reduce.5.cloned.1.call-done = (f32[2048]{0:T(1024)}, f32[2048]{0:T(1024)}, f32[2,2048]{1,0:T(2,128)}, f32[2048]{0:T(1024)}, f32[2048]{0:T(1024)}, /*index=5*/f32[2048]{0:T(1024)}, f32[8192]{0:T(1024)}, f32[2048]{0:T(1024)}) async-done(((f32[2048]{0:T(1024)}, f32[2048]{0:T(1024)}, f32[2,2048]{1,0:T(2,128)}, f32[2048]{0:T(1024)}, f32[2048]{0:T(1024)}, /*index=5*/f32[2048]{0:T(1024)}, f32[8192]{0:T(1024)}, ...) | async-done | bytes 98320 | tf_op jit(solution)/shard_map/psum | solution.py:272
  453.1 11.5 %convert_bitcast_fusion = bf16[2048,4096]{0,1:T(8,128)(2,1)} fusion(bf16[1,256,2048]{2,1,0:T(8,128)(2,1)S(1)} %copy-done.22, f32[256,4096]{1,0:T(8,128)} %copy-done.46), kind=kOutput, calls=%fused_computation.72 | convolution fusion | flops 4312793088 | bytes 22020096 | tf_op jit(solution)/shard_map/dot_general | solution.py:20
  464.6 21.7 %copy.68 = bf16[2048,4096]{1,0:T(8,128)(2,1)} copy(bf16[2048,4096]{0,1:T(8,128)(2,1)} %convert_bitcast_fusion) | data formatting | bytes 33554432
  487.7 9.8 convolution_convert_fusion
  498.7 8.0 convolution_convert_fusion.1
  506.7 23.5 %reduce-scatter.27.cloned.1.call-done = bf16[128,1024]{1,0:T(8,128)(2,1)} async-done(((bf16[2048,1024]{1,0:T(8,128)(2,1)}), bf16[128,1024]{1,0:T(8,128)(2,1)}) %reduce-scatter.27.cloned.1.call-update) | async-done | bytes 262160 | tf_op jit(solution)/shard_map/reduce_scatter | solution.py:253
  534.3 32.9 %all-reduce.7.cloned.1.call-done = (f32[2048]{0:T(1024)}, f32[2048]{0:T(1024)}, f32[2,2048]{1,0:T(2,128)}, f32[2048]{0:T(1024)}, f32[2048]{0:T(1024)}, /*index=5*/f32[2048]{0:T(1024)}, f32[8192]{0:T(1024)}, f32[2048]{0:T(1024)}) async-done(((f32[2048]{0:T(1024)}, f32[2048]{0:T(1024)}, f32[2,2048]{1,0:T(2,128)}, f32[2048]{0:T(1024)}, f32[2048]{0:T(1024)}, /*index=5*/f32[2048]{0:T(1024)}, f32[8192]{0:T(1024)}, ...) | async-done | bytes 98320 | tf_op jit(solution)/shard_map/psum | solution.py:271
  569.8 180.3 %reduce-scatter.31.cloned.1.call-done = bf16[128,4096]{1,0:T(8,128)(2,1)} async-done(((bf16[2048,4096]{1,0:T(8,128)(2,1)}), bf16[128,4096]{1,0:T(8,128)(2,1)}) %reduce-scatter.31.cloned.1.call-update) | async-done | bytes 1048592
  753.5 178.8 %reduce-scatter.29.cloned.1.call-done = bf16[128,4096]{1,0:T(8,128)(2,1)} async-done(((bf16[2048,4096]{1,0:T(8,128)(2,1)}), bf16[128,4096]{1,0:T(8,128)(2,1)}) %reduce-scatter.29.cloned.1.call-update) | async-done | bytes 1048592 | tf_op jit(solution)/shard_map/reduce_scatter | solution.py:256
  935.1 135.3 %reduce-scatter.25.cloned.1.call-done = bf16[128,3,1024]{2,0,1:T(8,128)(2,1)} async-done(((bf16[2048,3,1024]{2,0,1:T(8,128)(2,1)}), bf16[128,3,1024]{2,0,1:T(8,128)(2,1)}) %reduce-scatter.25.cloned.1.call-update) | async-done | bytes 786448 | tf_op jit(solution)/shard_map/reduce_scatter | solution.py:250
  (282 shorter events, 147.3 us)
Async XLA Ops:
  7.2 39.8 %all-gather.7.cloned.1.call-start = ((), (), s32[]{:S(2)}) async-start(), calls=%async_computation.11 | async-start | bytes 2621440 | tf_op jit(solution)/shard_map/all_gather | solution.py:75
  21.5 50.2 %all-gather.5.cloned.1.call-start = ((), (), s32[]{:S(2)}) async-start(), calls=%async_computation.10 | async-start | bytes 2621440 | tf_op jit(solution)/shard_map/all_gather | solution.py:76
  24.6 100.1 %reduce-scatter.13.cloned.1.call-start = ((), (), s32[]{:S(2)}) async-start(), calls=%async_computation.12 | async-start | bytes 1572864 | tf_op jit(solution)/shard_map/reduce_scatter | solution.py:130
  104.3 23.1 %copy-start.29 = (bf16[4096]{0:T(1024)(128)(2,1)S(1)}, bf16[4096]{0:T(1024)(128)(2,1)}, u32[]{:S(2)}) copy-start(bf16[4096]{0:T(1024)(128)(2,1)} %param.32) | copy-start | bytes 24580
  104.3 44.5 %all-gather.9.cloned.1.call-start = ((), (), s32[]{:S(2)}) async-start(), calls=%async_computation.13 | async-start | bytes 1572864 | tf_op jit(solution)/shard_map/all_gather | solution.py:138
  104.7 52.6 %copy-start.7 = (f32[1,256,2048]{2,1,0:T(8,128)}, f32[1,256,2048]{2,1,0:T(8,128)S(1)}, u32[]{:S(2)}) copy-start(f32[1,256,2048]{2,1,0:T(8,128)S(1)} %convert_element_type.219) | copy-start | bytes 6291460
  127.3 75.1 %reduce-scatter.17.cloned.1.call-start = ((), (), s32[]{:S(2)}) async-start(), calls=%async_computation.15 | async-start | bytes 1572864 | tf_op jit(solution)/shard_map/reduce_scatter | solution.py:161
  182.0 42.9 %reduce-scatter.15.cloned.1.call-start = ((), (), s32[]{:S(2)}) async-start(), calls=%async_computation.14 | async-start | bytes 1572864 | tf_op jit(solution)/shard_map/reduce_scatter | solution.py:144
  195.6 29.3 %copy-start.21 = (bf16[1,256,2048]{2,1,0:T(8,128)(2,1)S(1)}, bf16[1,256,2048]{2,1,0:T(8,128)(2,1)}, u32[]{:S(2)}) copy-start(bf16[1,256,2048]{2,1,0:T(8,128)(2,1)} %param.35) | copy-start | bytes 3145732
  195.6 55.8 %all-gather.11.cloned.1.call-start = ((), (), s32[]{:S(2)}) async-start(), calls=%async_computation.16 | async-start | bytes 1572864 | tf_op jit(solution)/shard_map/all_gather | solution.py:170
  204.5 25.8 %copy-start.13 = (f32[256,8,128]{0,2,1:T(8,128)S(1)}, f32[256,8,128]{0,2,1:T(8,128)}, u32[]{:S(2)}) copy-start(f32[256,8,128]{0,2,1:T(8,128)} %get-tuple-element.946) | copy-start | bytes 3145732
  229.9 98.5 %reduce-scatter.21.cloned.1.call-start = ((), (), s32[]{:S(2)}) async-start(), calls=%async_computation.18 | async-start | bytes 2621440 | tf_op jit(solution)/shard_map/reduce_scatter | solution.py:222
  296.9 65.5 %reduce-scatter.19.cloned.1.call-start = ((), (), s32[]{:S(2)}) async-start(), calls=%async_computation.17 | async-start | bytes 2621440 | tf_op jit(solution)/shard_map/reduce_scatter | solution.py:219
  300.9 93.7 %reduce-scatter.23.cloned.1.call-start = ((), (), s32[]{:S(2)}) async-start(), calls=%async_computation.19 | async-start | bytes 1572864 | tf_op jit(solution)/shard_map/reduce_scatter | solution.py:238
  301.7 72.4 %copy-start.17 = (bf16[256,1,1024]{2,0,1:T(8,128)(2,1)}, bf16[256,1,1024]{2,0,1:T(8,128)(2,1)S(1)}, u32[]{:S(2)}) copy-start(bf16[256,1,1024]{2,0,1:T(8,128)(2,1)S(1)} %copy.66) | copy-start | bytes 1572868
  330.0 44.1 %copy-start.18 = (bf16[256,1,1024]{2,0,1:T(8,128)(2,1)}, bf16[256,1,1024]{2,0,1:T(8,128)(2,1)S(1)}, u32[]{:S(2)}) copy-start(bf16[256,1,1024]{2,0,1:T(8,128)(2,1)S(1)} %stack_reshape.14) | copy-start | bytes 1572868
  374.1 78.9 %all-reduce.5.cloned.1.call-start = ((), (), s32[]{:S(2)}) async-start(), calls=%async_computation.24 | async-start | bytes 196608 | tf_op jit(solution)/shard_map/psum | solution.py:272
  374.4 24.6 %copy-start.14 = (bf16[256,2048]{1,0:T(8,128)(2,1)S(1)}, bf16[256,2048]{1,0:T(8,128)(2,1)}, u32[]{:S(2)}) copy-start(bf16[256,2048]{1,0:T(8,128)(2,1)} %all-gather.11.cloned.1.call-done) | copy-start | bytes 3145732
  376.6 22.3 %copy-start.26 = (f32[8192]{0:T(1024)}, f32[8192]{0:T(1024)S(1)}, u32[]{:S(2)}) copy-start(f32[8192]{0:T(1024)S(1)} %dynamic_update_slice.21) | copy-start | bytes 98308
  398.9 131.4 %reduce-scatter.27.cloned.1.call-start = ((), (), s32[]{:S(2)}) async-start(), calls=%async_computation.21 | async-start | bytes 4456448 | tf_op jit(solution)/shard_map/reduce_scatter | solution.py:253
  403.2 49.9 %copy-start.22 = (bf16[1,256,2048]{2,1,0:T(8,128)(2,1)S(1)}, bf16[1,256,2048]{2,1,0:T(8,128)(2,1)}, u32[]{:S(2)}) copy-start(bf16[1,256,2048]{2,1,0:T(8,128)(2,1)} %param.35) | copy-start | bytes 3145732
  403.3 163.9 %all-reduce.7.cloned.1.call-start = ((), (), s32[]{:S(2)}) async-start(), calls=%async_computation.25 | async-start | bytes 196608 | tf_op jit(solution)/shard_map/psum | solution.py:271
  453.0 297.1 %reduce-scatter.31.cloned.1.call-start = ((), (), s32[]{:S(2)}) async-start(), calls=%async_computation.23 | async-start | bytes 17825792
  486.3 446.0 %reduce-scatter.29.cloned.1.call-start = ((), (), s32[]{:S(2)}) async-start(), calls=%async_computation.22 | async-start | bytes 17825792 | tf_op jit(solution)/shard_map/reduce_scatter | solution.py:256
  497.5 572.9 %reduce-scatter.25.cloned.1.call-start = ((), (), s32[]{:S(2)}) async-start(), calls=%async_computation.20 | async-start | bytes 13369344 | tf_op jit(solution)/shard_map/reduce_scatter | solution.py:250
  506.7 25.4 %copy-start.12 = (f32[128,2048]{1,0:T(8,128)S(1)}, f32[128,2048]{1,0:T(8,128)}, u32[]{:S(2)}) copy-start(f32[128,2048]{1,0:T(8,128)} %copy-done.11) | copy-start | bytes 3145732
  751.8 321.1 %copy-start.37 = (f32[2048]{0:T(1024)S(1)}, f32[2048]{0:T(1024)}, u32[]{:S(2)}) copy-start(f32[2048]{0:T(1024)} %get-tuple-element.1328) | copy-start | bytes 24580
  751.8 321.7 %copy-start.36 = (f32[2048]{0:T(1024)S(1)}, f32[2048]{0:T(1024)}, u32[]{:S(2)}) copy-start(f32[2048]{0:T(1024)} %get-tuple-element.1329) | copy-start | bytes 24580
  751.8 322.2 %copy-start.35 = (f32[2048]{0:T(1024)S(1)}, f32[2048]{0:T(1024)}, u32[]{:S(2)}) copy-start(f32[2048]{0:T(1024)} %get-tuple-element.1333) | copy-start | bytes 24580
  751.8 322.8 %copy-start.34 = (f32[2048]{0:T(1024)S(1)}, f32[2048]{0:T(1024)}, u32[]{:S(2)}) copy-start(f32[2048]{0:T(1024)} %get-tuple-element.1334) | copy-start | bytes 24580
  751.8 323.4 %copy-start.33 = (f32[2048]{0:T(1024)S(1)}, f32[2048]{0:T(1024)}, u32[]{:S(2)}) copy-start(f32[2048]{0:T(1024)} %get-tuple-element.1335) | copy-start | bytes 24580
  751.8 324.0 %copy-start.32 = (f32[2048]{0:T(1024)S(1)}, f32[2048]{0:T(1024)}, u32[]{:S(2)}) copy-start(f32[2048]{0:T(1024)} %get-tuple-element.1339) | copy-start | bytes 24580
  (37 other events, 211.3 us)
Sparse Core Ops, SparseCore 0:
  21.7 25.2 all-gather.6
  49.1 22.5 all-gather.4
  104.4 20.2 reduce-scatter.12
  127.4 21.3 all-gather.8
  182.1 20.3 reduce-scatter.16
  204.5 20.3 reduce-scatter.14
  230.1 21.2 all-gather.10
  297.0 31.3 reduce-scatter.20
  331.0 31.4 reduce-scatter.18
  374.3 20.3 reduce-scatter.22
  399.7 53.2 all-reduce.4
  457.2 72.9 reduce-scatter.26
  533.1 34.0 all-reduce.6
  571.7 178.3 reduce-scatter.30
  754.7 177.5 reduce-scatter.28
  936.7 133.5 reduce-scatter.24
